TPU v7x, 32 devices: a whole 2x2x4 slice. The times are simulated.
32 devices in a mesh: groups: 2 (over x), row: 16 (over z, y, core).
Axes of the slice: x: 2, y: 2, z: 4, core: 2. Of those that a mesh axis runs over, the one named last changes fastest.
Arguments:
- features: bfloat16 [128, 64, 512], P(('groups', 'row')), parts along dimension 0, may hold values from -6 to 6
- cotangent: bfloat16 [128, 64, 512], P(('groups', 'row')), parts along dimension 0, may hold values from -6 to 6
- depth_weight: bfloat16 [49, 512], P(None, 'row'), may hold values from -0.875 to 0.875
- depth_bias: bfloat16 [512], P('row'), may hold values from -3 to 3
- norm_gain: bfloat16 [512], P('row'), may hold values from 0.25 to 1.75
- norm_shift: bfloat16 [512], P('row'), may hold values from -3 to 3
- up_weight: bfloat16 [512, 2048], P('row'), may hold values from -0.25 to 0.25
- up_bias: bfloat16 [2048], P('row'), may hold values from -3 to 3
- down_weight: bfloat16 [2048, 512], P('row'), may hold values from -0.125 to 0.125
- down_bias: bfloat16 [512], P('row'), may hold values from -3 to 3
Outputs:
- block_out: bfloat16 [128, 64, 512], P(('groups', 'row')), parts along dimension 0
- grad_features: bfloat16 [128, 64, 512], P(('groups', 'row')), parts along dimension 0
- grad_up_weight: float32 [1024, 2048], P(('groups', 'row')), parts along dimension 0
- grad_down_weight: float32 [4096, 512], P(('groups', 'row')), parts along dimension 0
- grad_depth_weight: float32 [98, 512], P('groups', 'row'), parts along dimension 0
- grad_depth_bias: float32 [1024], P(('groups', 'row')), parts along dimension 0
- grad_norm_gain: float32 [1024], P(('groups', 'row')), parts along dimension 0
- grad_norm_shift: float32 [1024], P(('groups', 'row')), parts along dimension 0
- grad_up_bias: float32 [4096], P(('groups', 'row')), parts along dimension 0
- grad_down_bias: float32 [1024], P(('groups', 'row')), parts along dimension 0
There are 2 independent parts, one for each index of `groups`. A program takes and returns all parts, laid end to end along the dimension named above; an argument that names none is the same for every part. Nothing has to cross between parts.
All inputs are finite; a program needn't handle non-finite values.
Results may differ from a plain program's by a relative error of at most 0.0055.
Values may be sent and summed in bfloat16 or wider, within the bound.
A program may use at most 64 MiB of HBM per device.

v0:
```python
import math
import jax
import jax.numpy as jnp
from jax import lax
from jax.sharding import PartitionSpec as P

eps = 1e-06


def with_halo(block, sides, width):
    for axis, dim in sides:
        count = lax.axis_size(axis)
        forward = [(i, i + 1) for i in range(count - 1)]
        backward = [(target, source) for source, target in forward]
        low = lax.ppermute(
            lax.slice_in_dim(block, block.shape[dim] - width, None, axis=dim), axis, forward
        )
        high = lax.ppermute(lax.slice_in_dim(block, 0, width, axis=dim), axis, backward)
        block = jnp.concatenate([low, block, high], axis=dim)
    return block


def gelu_value(value):
    return 0.5 * value * (1.0 + lax.erf(value * (1.0 / math.sqrt(2.0))))


def gelu_slope(value):
    cumulative = 0.5 * (1.0 + lax.erf(value * (1.0 / math.sqrt(2.0))))
    density = jnp.exp(-0.5 * value * value) * (1.0 / math.sqrt(2.0 * math.pi))
    return cumulative + value * density


def depth_conv(padded, kernel, height, width):
    total = jnp.zeros((height, width, kernel.shape[1]), jnp.float32)
    for first in range(7):
        for second in range(7):
            total = (
                total
                + padded[first : first + height, second : second + width, :]
                * kernel[first * 7 + second]
            )
    return total


def depth_conv_back(padded, kernel, height, width):
    total = jnp.zeros((height, width, kernel.shape[1]), jnp.float32)
    for first in range(7):
        for second in range(7):
            total = (
                total
                + padded[6 - first : 6 - first + height, 6 - second : 6 - second + width, :]
                * kernel[first * 7 + second]
            )
    return total


def per_device(
    features,
    cotangent,
    depth_weight,
    depth_bias,
    norm_gain,
    norm_shift,
    up_weight,
    up_bias,
    down_weight,
    down_bias,
):
    height, width, chans = features.shape
    devices = lax.axis_size("row")
    cells = height * width
    scale = 1.0 / math.sqrt(cells * devices)
    kernel, conv_bias, gain, shift, bias_down, bias_up = (
        lax.all_gather(depth_weight, "row", axis=1, tiled=True),
        lax.all_gather(depth_bias, "row", axis=0, tiled=True),
        lax.all_gather(norm_gain, "row", axis=0, tiled=True),
        lax.all_gather(norm_shift, "row", axis=0, tiled=True),
        lax.all_gather(down_bias, "row", axis=0, tiled=True),
        lax.all_gather(up_bias, "row", axis=0, tiled=True),
    )
    kernel = kernel.astype(jnp.float32)
    gain = gain.astype(jnp.float32)
    rimmed = with_halo(features, (("row", 0),), 3)
    padded = jnp.pad(rimmed.astype(jnp.float32), ((0, 0), (3, 3), (0, 0)))
    conv = depth_conv(padded, kernel, height, width) + conv_bias.astype(jnp.float32)
    mean_val = jnp.mean(conv, axis=2, keepdims=True)
    centered = conv - mean_val
    var_val = jnp.mean(centered * centered, axis=2, keepdims=True)
    inv = lax.rsqrt(var_val + eps)
    normed = centered * inv
    normal_out = (normed * gain + shift.astype(jnp.float32)).astype(jnp.bfloat16)
    flat_norm = normal_out.reshape(cells, chans)
    flat_cot = cotangent.reshape(cells, chans)
    columns = flat_norm
    hidden = jnp.dot(
        columns,
        lax.all_gather(up_weight, "row", axis=0, tiled=True),
        preferred_element_type=jnp.float32,
    ) + bias_up.astype(jnp.float32)
    act = gelu_value(hidden).astype(jnp.bfloat16)
    columns = act
    mixed = jnp.dot(
        columns,
        lax.all_gather(down_weight, "row", axis=0, tiled=True),
        preferred_element_type=jnp.float32,
    )
    block_out = (
        features.astype(jnp.float32)
        + (mixed + bias_down.astype(jnp.float32)).reshape(height, width, chans)
    ).astype(jnp.bfloat16)
    down_full = (
        lax.dot_general(act, flat_cot, (((0,), (0,)), ((), ())), preferred_element_type=jnp.float32)
        * scale
    )
    grad_down_weight = lax.psum_scatter(down_full, "row", scatter_dimension=0, tiled=True)
    dact = lax.dot_general(
        flat_cot,
        lax.all_gather(down_weight, "row", axis=0, tiled=True),
        (((1,), (1,)), ((), ())),
        preferred_element_type=jnp.float32,
    )
    dhidden = (dact * gelu_slope(hidden)).astype(jnp.bfloat16)
    columns = flat_norm
    grad_up_weight = lax.psum_scatter(
        lax.dot_general(
            columns, dhidden, (((0,), (0,)), ((), ())), preferred_element_type=jnp.float32
        )
        * scale,
        "row",
        scatter_dimension=0,
        tiled=True,
    )
    dnorm = lax.dot_general(
        dhidden,
        lax.all_gather(up_weight, "row", axis=0, tiled=True),
        (((1,), (1,)), ((), ())),
        preferred_element_type=jnp.float32,
    )
    dnorm = dnorm.reshape(height, width, chans)
    down_bias_term = jnp.sum(flat_cot.astype(jnp.float32), axis=0) * scale
    up_bias_term = jnp.sum(dhidden.astype(jnp.float32), axis=0) * scale
    gain_term = jnp.sum(dnorm * normed, axis=(0, 1)) * scale
    shift_term = jnp.sum(dnorm, axis=(0, 1)) * scale
    grad_down_bias, grad_up_bias, grad_norm_gain, grad_norm_shift = (
        lax.psum_scatter(down_bias_term, "row", scatter_dimension=0, tiled=True),
        lax.psum_scatter(up_bias_term, "row", scatter_dimension=0, tiled=True),
        lax.psum_scatter(gain_term, "row", scatter_dimension=0, tiled=True),
        lax.psum_scatter(shift_term, "row", scatter_dimension=0, tiled=True),
    )
    scaled = dnorm * gain
    dconv = inv * (
        scaled
        - jnp.mean(scaled, axis=2, keepdims=True)
        - normed * jnp.mean(scaled * normed, axis=2, keepdims=True)
    )
    dconv = dconv.astype(jnp.bfloat16)
    dconv_wide = dconv.astype(jnp.float32)
    back_rim = with_halo(dconv, (("row", 0),), 3)
    back_pad = jnp.pad(back_rim.astype(jnp.float32), ((0, 0), (3, 3), (0, 0)))
    grad_features = (
        cotangent.astype(jnp.float32) + depth_conv_back(back_pad, kernel, height, width)
    ).astype(jnp.bfloat16)
    taps = []
    for first in range(7):
        for second in range(7):
            taps.append(
                jnp.sum(
                    dconv_wide * padded[first : first + height, second : second + width, :],
                    axis=(0, 1),
                )
            )
    kernel_term = jnp.stack(taps, axis=0) * scale
    conv_bias_term = jnp.sum(dconv_wide, axis=(0, 1)) * scale
    grad_depth_weight, grad_depth_bias = (
        lax.psum_scatter(kernel_term, "row", scatter_dimension=1, tiled=True),
        lax.psum_scatter(conv_bias_term, "row", scatter_dimension=0, tiled=True),
    )
    return (
        block_out,
        grad_features,
        grad_up_weight,
        grad_down_weight,
        grad_depth_weight,
        grad_depth_bias,
        grad_norm_gain,
        grad_norm_shift,
        grad_up_bias,
        grad_down_bias,
    )


def solution(mesh):
    placed = (
        P(("groups", "row"), None, None),
        P(("groups", "row"), None, None),
        P(None, "row"),
        P("row"),
        P("row"),
        P("row"),
        P("row", None),
        P("row"),
        P("row", None),
        P("row"),
    )
    return jax.shard_map(
        per_device,
        mesh=mesh,
        in_specs=placed,
        out_specs=(
            P(("groups", "row"), None, None),
            P(("groups", "row"), None, None),
            P(("groups", "row"), None),
            P(("groups", "row"), None),
            P("groups", "row"),
            P(("groups", "row")),
            P(("groups", "row")),
            P(("groups", "row")),
            P(("groups", "row")),
            P(("groups", "row")),
        ),
        check_vma=False,
    )
```

profile of v0, /device:TPU:0, one launch (start us, length us, event | category | flops | bytes accessed | tf_op | source)
XLA Modules:
  0.0 336.8 jit_solution(5923359344454385601)
XLA Ops:
  8.0 0.7 all-gather.6.cloned.1.call-update
  8.7 1.1 fusion.148
  9.8 2.4 collective-permute-start
  12.2 1.3 collective-permute-start.1
  13.5 25.6 %all_gather.26 = bf16[49,512]{0,1:T(8,128)(2,1)S(1)} all-gather(bf16[49,32]{0,1:T(8,128)(2,1)} %param.12), channel_id=1, replica_groups=mesh['groups'=2,'row'=16] {'row'}, dimensions={1}, use_global_device_ids=true | all-gather | bytes 53312 | tf_op jit(solution)/shard_map/all_gather | solution.py:74
  39.1 2.6 slice_reduce_fusion.48
  41.8 1.6 slice_reduce_fusion.46
  45.7 30.5 %all-reduce.12 = (bf16[512]{0:T(512)(128)(2,1)S(1)}, bf16[512]{0:T(512)(128)(2,1)S(1)}, bf16[512]{0:T(512)(128)(2,1)S(1)}, bf16[512]{0:T(512)(128)(2,1)}) all-reduce(bf16[512]{0:T(512)(128)(2,1)S(1)} %dynamic-update-slice, bf16[512]{0:T(512)(128)(2,1)S(1)} %dynamic-update-slice.2, ...), channel_id=1, replica_groups=mesh['groups'=2,'row'=16] {'row'}, use_global_device_ids=true, to_apply=%add.2 | all-reduce | flops 2048 | bytes 8192
  76.2 17.5 %all-gather = bf16[16,1,128]{2,1,0:T(2,128)(2,1)S(1)} all-gather(bf16[1,1,128]{2,1,0:T(2,128)(2,1)S(1)} %bitcast.131), channel_id=1, replica_groups=mesh['groups'=2,'row'=16] {'row'}, dimensions={0}, use_global_device_ids=true | all-gather | bytes 4352 | tf_op jit(solution)/shard_map/all_gather | solution.py:79
  93.8 2.7 slice_reduce_fusion.47
  96.8 4.7 %fusion.146 = (f32[4,64]{1,0:T(4,128)S(1)}, f32[4,64,512]{2,1,0:T(8,128)S(1)}) fusion(f32[512]{0:T(512)S(1)} %convert_element_type.62, f32[512]{0:T(512)S(1)} %get-tuple-element.85, f32[512]{0:T(512)S(1)} %get-tuple-element.86, f32[512]{0:T(512)S(1)} %get-tuple-element.87, f32[512]{0:T(512)S(1)} %get-tuple-element.88, ...), kind=kLoop, calls=%fused_computation.368 | loop fusion | flops 12975872 | bytes 5608448 | tf_op jit(solution)/shard_map/reduce_sum | solution.py:86
  102.1 3.8 %multiply_convert_fusion = (bf16[256,2048]{1,0:T(8,128)(2,1)S(1)}, f32[256,2048]{1,0:T(8,128)}) fusion(f32[2048]{0:T(1024)S(1)} %bitcast.81, bf16[256,512]{1,0:T(8,128)(2,1)S(1)} %bitcast.75, bf16[512,2048]{1,0:T(8,128)(2,1)} %all-gather.4.cloned.1.call-done), kind=kOutput, calls=%fused_computation.61 | convolution fusion | flops 540016640 | bytes 5513216 | tf_op jit(solution)/shard_map/dot_general | solution.py:95
  106.0 4.2 %convert_reduce_fusion.1 = (f32[2048]{0:T(1024)}, bf16[256,2048]{1,0:T(8,128)(2,1)S(1)}) fusion(f32[256,2048]{1,0:T(8,128)} %get-tuple-element.152, bf16[256,512]{1,0:T(8,128)(2,1)} %bitcast.77, bf16[2048,512]{1,0:T(8,128)(2,1)} %all-gather.6.cloned.1.call-done), kind=kOutput, calls=%fused_computation.60 | convolution fusion | flops 543160320 | bytes 5513216 | tf_op jit(solution)/shard_map/dot_general | solution.py:116
  110.2 1.3 fusion.145
  111.5 0.8 copy-done
  112.3 0.8 multiply_reduce_fusion
  114.4 3.2 fusion.143
  117.5 1.4 fusion.142
  119.1 1.0 fusion.144
  120.3 2.3 stack.199
  122.6 0.9 copy.22
  123.8 3.9 %convolution_multiply_fusion.1 = f32[512,2048]{1,0:T(8,128)} fusion(bf16[256,512]{1,0:T(8,128)(2,1)S(1)} %bitcast.76, bf16[256,2048]{1,0:T(8,128)(2,1)} %copy-done.6), kind=kOutput, calls=%fused_computation.51 | convolution fusion | flops 537919488 | bytes 5505024 | tf_op jit(solution)/shard_map/dot_general | solution.py:125
  127.7 0.9 copy-done.4
  128.6 2.7 convolution_multiply_fusion
  132.8 59.3 %all-reduce.11 = (f32[512]{0:T(512)S(1)}, f32[512]{0:T(512)S(1)}, f32[512]{0:T(512)S(1)}, f32[2048]{0:T(1024)S(1)}, f32[512]{0:T(512)S(1)}) all-reduce(f32[512]{0:T(512)S(1)} %broadcast_multiply_fusion.5, f32[512]{0:T(512)S(1)} %get-tuple-element.157, ...), channel_id=5, replica_groups=mesh['groups'=2,'row'=16] {'row'}, use_global_device_ids=true, to_apply=%region_57.58.clone | all-reduce | flops 4096 | bytes 32768
  194.5 1.3 collective-permute-start.2
  195.8 1.3 collective-permute-start.3
  197.7 2.4 convolution_add_fusion.1
  200.3 0.8 add_convert_fusion
  201.4 4.7 %fusion.5 = bf16[4,64,512]{2,1,0:T(8,128)(2,1)} fusion(bf16[4,64,512]{2,1,0:T(8,128)(2,1)S(1)} %copy-done.4, f32[10,64,512]{2,1,0:T(8,128)S(1)} %maximum_convert_fusion.1, f32[512]{0:T(512)S(1)} %get-tuple-element.85, f32[512]{0:T(512)S(1)} %get-tuple-element.86, f32[512]{0:T(512)S(1)} %get-tuple-element.87, f32[512]{0:T(512)S(1)} %get-tuple-element.88, ...), kind=kLoop, calls=%fused_computation.152 | loop fusion | flops 13107200 | bytes 5605376 | tf_op jit(solution)/shard_map/convert_element_type | solution.py:162
  206.0 48.2 %reduce-scatter.6.cloned.1.call-done = f32[32,2048]{1,0:T(8,128)} async-done(((f32[512,2048]{1,0:T(8,128)}), f32[32,2048]{1,0:T(8,128)}) %reduce-scatter.6.cloned.1.call-update) | async-done | bytes 262160 | tf_op jit(solution)/shard_map/reduce_scatter | solution.py:124
  254.2 76.1 %reduce-scatter.8.cloned.1.call-done = f32[128,512]{1,0:T(8,128)} async-done(((f32[2048,512]{1,0:T(8,128)}), f32[128,512]{1,0:T(8,128)}) %reduce-scatter.8.cloned.1.call-update) | async-done | bytes 262160 | tf_op jit(solution)/shard_map/reduce_scatter | solution.py:115
  (190 shorter events, 8.0 us)
Async XLA Ops:
  7.2 94.9 %all-gather.4.cloned.1.call-start = ((), (), s32[]{:S(2)}) async-start(), calls=%async_computation.3 | async-start | bytes 2228224 | tf_op jit(solution)/shard_map/all_gather | solution.py:97
  7.9 98.0 %all-gather.6.cloned.1.call-start = ((), (), s32[]{:S(2)}) async-start(), calls=%async_computation.4 | async-start | bytes 2228224 | tf_op jit(solution)/shard_map/all_gather | solution.py:104
  8.7 197.4 %reduce-scatter.10.cloned.1.call-start = ((), (), s32[]{:S(2)}) async-start(), calls=%async_computation.7 | async-start | bytes 278528
  9.8 86.9 %collective-permute-start = (bf16[3,64,512]{2,1,0:T(8,128)(2,1)S(1)}, bf16[3,64,512]{2,1,0:T(8,128)(2,1)S(1)}, u32[]{:S(2)}, u32[]{:S(2)}) collective-permute-start(bf16[3,64,512]{2,1,0:T(8,128)(2,1)S(1)} %get-tuple-element.147), channel_id=1, source_target_pairs={{0,1},{1,2},{2,3},{3,4},{4,5},{5,6},{6,7},{7,8},{8,9},{9,10},{10,1... | collective-permute-start | bytes 589832 | tf_op jit(solution)/shard_map/ppermute | solution.py:15
  12.2 84.5 %collective-permute-start.1 = (bf16[3,64,512]{2,1,0:T(8,128)(2,1)S(1)}, bf16[3,64,512]{2,1,0:T(8,128)(2,1)S(1)}, u32[]{:S(2)}, u32[]{:S(2)}) collective-permute-start(bf16[3,64,512]{2,1,0:T(8,128)(2,1)S(1)} %get-tuple-element.148), channel_id=1, source_target_pairs={{1,0},{2,1},{3,2},{4,3},{5,4},{6,5},{7,6},{8,7},{9,8},{10,9},{11,1... | collective-permute-start | bytes 589832 | tf_op jit(solution)/shard_map/ppermute | solution.py:18
  41.8 3.7 %copy-start.69 = (bf16[32]{0:T(256)(128)(2,1)S(1)}, bf16[32]{0:T(256)(128)(2,1)}, u32[]{:S(2)}) copy-start(bf16[32]{0:T(256)(128)(2,1)} %param.19) | copy-start | bytes 196
  41.8 34.4 %copy-start.65 = (bf16[128]{0:T(256)(128)(2,1)S(1)}, bf16[128]{0:T(256)(128)(2,1)}, u32[]{:S(2)}) copy-start(bf16[128]{0:T(256)(128)(2,1)} %param.17) | copy-start | bytes 772
  96.5 5.0 %copy-start.7 = (f32[512]{0:T(512)}, f32[512]{0:T(512)S(1)}, u32[]{:S(2)}) copy-start(f32[512]{0:T(512)S(1)} %get-tuple-element.104) | copy-start | bytes 6148
  96.5 5.0 %copy-start.9 = (f32[512]{0:T(512)}, f32[512]{0:T(512)S(1)}, u32[]{:S(2)}) copy-start(f32[512]{0:T(512)S(1)} %get-tuple-element.105) | copy-start | bytes 6148
  96.5 5.0 %copy-start.11 = (f32[512]{0:T(512)}, f32[512]{0:T(512)S(1)}, u32[]{:S(2)}) copy-start(f32[512]{0:T(512)S(1)} %get-tuple-element.106) | copy-start | bytes 6148
  96.5 5.0 %copy-start.13 = (f32[512]{0:T(512)}, f32[512]{0:T(512)S(1)}, u32[]{:S(2)}) copy-start(f32[512]{0:T(512)S(1)} %get-tuple-element.107) | copy-start | bytes 6148
  96.5 5.0 %copy-start.15 = (f32[512]{0:T(512)}, f32[512]{0:T(512)S(1)}, u32[]{:S(2)}) copy-start(f32[512]{0:T(512)S(1)} %get-tuple-element.108) | copy-start | bytes 6148
  96.5 5.0 %copy-start.17 = (f32[512]{0:T(512)}, f32[512]{0:T(512)S(1)}, u32[]{:S(2)}) copy-start(f32[512]{0:T(512)S(1)} %get-tuple-element.109) | copy-start | bytes 6148
  96.5 5.0 %copy-start.19 = (f32[512]{0:T(512)}, f32[512]{0:T(512)S(1)}, u32[]{:S(2)}) copy-start(f32[512]{0:T(512)S(1)} %get-tuple-element.110) | copy-start | bytes 6148
  96.5 5.0 %copy-start.21 = (f32[512]{0:T(512)}, f32[512]{0:T(512)S(1)}, u32[]{:S(2)}) copy-start(f32[512]{0:T(512)S(1)} %get-tuple-element.111) | copy-start | bytes 6148
  96.6 5.0 %copy-start.23 = (f32[512]{0:T(512)}, f32[512]{0:T(512)S(1)}, u32[]{:S(2)}) copy-start(f32[512]{0:T(512)S(1)} %get-tuple-element.112) | copy-start | bytes 6148
  96.6 5.0 %copy-start.25 = (f32[512]{0:T(512)}, f32[512]{0:T(512)S(1)}, u32[]{:S(2)}) copy-start(f32[512]{0:T(512)S(1)} %get-tuple-element.113) | copy-start | bytes 6148
  96.6 5.0 %copy-start.27 = (f32[512]{0:T(512)}, f32[512]{0:T(512)S(1)}, u32[]{:S(2)}) copy-start(f32[512]{0:T(512)S(1)} %get-tuple-element.114) | copy-start | bytes 6148
  96.6 5.0 %copy-start.29 = (f32[512]{0:T(512)}, f32[512]{0:T(512)S(1)}, u32[]{:S(2)}) copy-start(f32[512]{0:T(512)S(1)} %get-tuple-element.115) | copy-start | bytes 6148
  96.6 5.0 %copy-start.31 = (f32[512]{0:T(512)}, f32[512]{0:T(512)S(1)}, u32[]{:S(2)}) copy-start(f32[512]{0:T(512)S(1)} %get-tuple-element.116) | copy-start | bytes 6148
  96.6 5.0 %copy-start.33 = (f32[512]{0:T(512)}, f32[512]{0:T(512)S(1)}, u32[]{:S(2)}) copy-start(f32[512]{0:T(512)S(1)} %get-tuple-element.117) | copy-start | bytes 6148
  96.6 5.0 %copy-start.35 = (f32[512]{0:T(512)}, f32[512]{0:T(512)S(1)}, u32[]{:S(2)}) copy-start(f32[512]{0:T(512)S(1)} %get-tuple-element.118) | copy-start | bytes 6148
  96.6 5.0 %copy-start.37 = (f32[512]{0:T(512)}, f32[512]{0:T(512)S(1)}, u32[]{:S(2)}) copy-start(f32[512]{0:T(512)S(1)} %get-tuple-element.119) | copy-start | bytes 6148
  96.6 5.0 %copy-start.39 = (f32[512]{0:T(512)}, f32[512]{0:T(512)S(1)}, u32[]{:S(2)}) copy-start(f32[512]{0:T(512)S(1)} %get-tuple-element.120) | copy-start | bytes 6148
  96.7 5.0 %copy-start.41 = (f32[512]{0:T(512)}, f32[512]{0:T(512)S(1)}, u32[]{:S(2)}) copy-start(f32[512]{0:T(512)S(1)} %get-tuple-element.121) | copy-start | bytes 6148
  102.1 3.9 %copy-start.2 = (bf16[4,64,512]{2,1,0:T(8,128)(2,1)}, bf16[4,64,512]{2,1,0:T(8,128)(2,1)S(1)}, u32[]{:S(2)}) copy-start(bf16[4,64,512]{2,1,0:T(8,128)(2,1)S(1)} %add_convert_fusion.1) | copy-start | bytes 786436
  106.0 4.2 %copy-start.5 = (bf16[512,2048]{1,0:T(8,128)(2,1)S(1)}, bf16[512,2048]{1,0:T(8,128)(2,1)}, u32[]{:S(2)}) copy-start(bf16[512,2048]{1,0:T(8,128)(2,1)} %all-gather.4.cloned.1.call-done) | copy-start | bytes 6291460
  119.1 4.7 %copy-start.3 = (bf16[4,64,512]{2,1,0:T(8,128)(2,1)S(1)}, bf16[4,64,512]{2,1,0:T(8,128)(2,1)}, u32[]{:S(2)}) copy-start(bf16[4,64,512]{2,1,0:T(8,128)(2,1)} %copy-done.2) | copy-start | bytes 786436
  123.5 130.7 %reduce-scatter.6.cloned.1.call-start = ((), (), s32[]{:S(2)}) async-start(), calls=%async_computation.5 | async-start | bytes 4456448 | tf_op jit(solution)/shard_map/reduce_scatter | solution.py:124
  127.7 202.6 %reduce-scatter.8.cloned.1.call-start = ((), (), s32[]{:S(2)}) async-start(), calls=%async_computation.6 | async-start | bytes 4456448 | tf_op jit(solution)/shard_map/reduce_scatter | solution.py:115
  194.5 6.6 %collective-permute-start.2 = (bf16[3,64,512]{2,1,0:T(8,128)(2,1)S(1)}, bf16[3,64,512]{2,1,0:T(8,128)(2,1)S(1)}, u32[]{:S(2)}, u32[]{:S(2)}) collective-permute-start(bf16[3,64,512]{2,1,0:T(8,128)(2,1)S(1)} %get-tuple-element.145), channel_id=1, source_target_pairs={{0,1},{1,2},{2,3},{3,4},{4,5},{5,6},{6,7},{7,8},{8,9},{9,10},{10,1... | collective-permute-start | bytes 589832 | tf_op jit(solution)/shard_map/ppermute | solution.py:15
  195.8 5.3 %collective-permute-start.3 = (bf16[3,64,512]{2,1,0:T(8,128)(2,1)S(1)}, bf16[3,64,512]{2,1,0:T(8,128)(2,1)S(1)}, u32[]{:S(2)}, u32[]{:S(2)}) collective-permute-start(bf16[3,64,512]{2,1,0:T(8,128)(2,1)S(1)} %get-tuple-element.146), channel_id=1, source_target_pairs={{1,0},{2,1},{3,2},{4,3},{5,4},{6,5},{7,6},{8,7},{9,8},{10,9},{11,1... | collective-permute-start | bytes 589832 | tf_op jit(solution)/shard_map/ppermute | solution.py:18
  (47 other events, 64.7 us)
Sparse Core Ops, SparseCore 0:
  10.1 44.2 all-gather.3
  56.6 40.1 all-gather.5
  123.6 54.3 reduce-scatter.9
  182.2 71.8 reduce-scatter.5
  258.4 71.7 reduce-scatter.7
where the time goes:
time: 337 us
  blocking collectives  133 us (39%)
  waiting for transfers between devices  126 us (37%)
  matrix products  18.4 us (5%)
  local copies, waits for them, and re-layouts  18.3 us (5%)
  other arithmetic  17.8 us (5%)
  between operations  16.9 us (5%)
  starting transfers between devices  6.71 us (2%)
    unnamed x2, blocking collectives  89.8 us
    reduce_scatter x1, waiting for transfers between devices, per_device(): lax.psum_scatter(down_full, 'row', scatter_dimension=0, tiled=True)  76.1 us
    reduce_scatter x1, waiting for transfers between devices, per_device(): lax.psum_scatter(lax.dot_general(columns, dhidden, (((0,), (0,)), ((), ()...  48.2 us
    all_gather x1, blocking collectives, per_device(): lax.all_gather(depth_weight, 'row', axis=1, tiled=True)  25.6 us
    all_gather x1, blocking collectives, per_device(): lax.all_gather(up_bias, 'row', axis=0, tiled=True)  17.5 us
    unnamed x155, local copies, waits for them, and re-layouts  7.34 us
    slice x3, local copies, waits for them, and re-layouts, depth_conv(): kernel[first * 7 + second]  6.92 us
  transfers between devices with their start and end apart: 9, of which 2 were waited for; matrix products, arithmetic and copies ran while one was open for 11% of the time, Pallas kernels for 0%

commit v1 on v0

--- a/solution.py
+++ b/solution.py
@@ -5,6 +5,40 @@
 from jax.sharding import PartitionSpec as P
 
 eps = 1e-06
+
+
+def launch_domain_on(local_block, dim_at):
+    row_out, y_new, k_now = (lax.axis_size("row"), lax.axis_index("row"), local_block.shape[dim_at])
+    y1 = lax.dynamic_update_slice_in_dim(
+        jnp.zeros(
+            [
+                dev_i * row_out if tick == dim_at else dev_i
+                for tick, dev_i in enumerate(local_block.shape)
+            ],
+            local_block.dtype,
+        ),
+        local_block,
+        y_new * k_now,
+        axis=dim_at,
+    )
+    block_last = carry_out = local_block
+    for k0 in range(1, row_out // 2 + 1):
+        block_last = lax.ppermute(
+            block_last, "row", list(map(lambda tick: (tick, (tick + 1) % row_out), range(row_out)))
+        )
+        y1 = lax.dynamic_update_slice_in_dim(
+            y1, block_last, (y_new - k0) % row_out * k_now, axis=dim_at
+        )
+        if 2 * k0 < row_out:
+            carry_out = lax.ppermute(
+                carry_out,
+                "row",
+                list(map(lambda tick: (tick, (tick - 1) % row_out), range(row_out))),
+            )
+            y1 = lax.dynamic_update_slice_in_dim(
+                y1, carry_out, (y_new + k0) % row_out * k_now, axis=dim_at
+            )
+    return y1
 
 
 def with_halo(block, sides, width):
@@ -76,7 +110,7 @@
         lax.all_gather(norm_gain, "row", axis=0, tiled=True),
         lax.all_gather(norm_shift, "row", axis=0, tiled=True),
         lax.all_gather(down_bias, "row", axis=0, tiled=True),
-        lax.all_gather(up_bias, "row", axis=0, tiled=True),
+        launch_domain_on(up_bias, 0),
     )
     kernel = kernel.astype(jnp.float32)
     gain = gain.astype(jnp.float32)

time: 337 us -> 360 us (1.068)
  starting transfers between devices: 6.71 us -> 37.7 us
  blocking collectives: 133 us -> 111 us
  waiting for transfers between devices: 126 us -> 136 us
    ppermute x0 -> x15, starting transfers between devices: none -> 32.1 us  [the longest x7 31.5 us: launch_domain_on(): lax.ppermute(carry_out, 'row', list(map(lambda tick: (tick, (tick - 1) %...]
    all_gather x1 -> x0, blocking collectives: 17.5 us -> none  [per_device(): lax.all_gather(up_bias, 'row', axis=0, tiled=True)]
    ppermute x0 -> x15, waiting for transfers between devices: none -> 10.4 us  [the longest x8 10.1 us: launch_domain_on(): lax.ppermute(block_last, 'row', list(map(lambda tick: (tick, (tick + 1) %...]
  transfers between devices with their start and end apart: 9 -> 24, of which waited for: 2 -> 13; matrix products, arithmetic and copies ran while one was open for 11% -> 11% of each run, Pallas kernels for 0% -> 0%
where the time goes in v1:
time: 360 us
  waiting for transfers between devices  136 us (38%)
  blocking collectives  111 us (31%)
  starting transfers between devices  37.7 us (10%)
  local copies, waits for them, and re-layouts  21.4 us (6%)
  matrix products  18.4 us (5%)
  other arithmetic  17.8 us (5%)
  between operations  17.2 us (5%)
    unnamed x2, blocking collectives  88.2 us
    reduce_scatter x1, waiting for transfers between devices, per_device(): lax.psum_scatter(down_full, 'row', scatter_dimension=0, tiled=True)  76 us
    reduce_scatter x1, waiting for transfers between devices, per_device(): lax.psum_scatter(lax.dot_general(columns, dhidden, (((0,), (0,)), ((), ()...  48.3 us
    ppermute x7, starting transfers between devices, launch_domain_on(): lax.ppermute(carry_out, 'row', list(map(lambda tick: (tick, (tick - 1) %...  31.5 us
    all_gather x1, blocking collectives, per_device(): lax.all_gather(depth_weight, 'row', axis=1, tiled=True)  23 us
    ppermute x8, waiting for transfers between devices, launch_domain_on(): lax.ppermute(block_last, 'row', list(map(lambda tick: (tick, (tick + 1) %...  10.1 us
    unnamed x155, local copies, waits for them, and re-layouts  7.34 us
  transfers between devices with their start and end apart: 24, of which 13 were waited for; matrix products, arithmetic and copies ran while one was open for 11% of the time, Pallas kernels for 0%

profile of v1, /device:TPU:0, one launch (start us, length us, event | category | flops | bytes accessed | tf_op | source)
XLA Modules:
  0.0 359.8 jit_solution(12890754750236040812)
XLA Ops:
  9.2 5.0 %collective-permute-start.3 = (bf16[128]{0:T(256)(128)(2,1)}, bf16[128]{0:T(256)(128)(2,1)S(1)}, u32[]{:S(2)}, u32[]{:S(2)}) collective-permute-start(bf16[128]{0:T(256)(128)(2,1)} %param.17), channel_id=1, source_target_pairs={{0,15},{1,0},{2,1},{3,2},{4,3},{5,4},{6,5},{7,6},{8,7},{9,8},{10,9... | collective-permute-start | bytes 776 | tf_op jit(solution)/shard_map/ppermute | solution.py:33
  15.3 1.3 collective-permute-start
  16.7 1.3 collective-permute-start.1
  18.0 23.0 %all_gather.23 = bf16[49,512]{0,1:T(8,128)(2,1)S(1)} all-gather(bf16[49,32]{0,1:T(8,128)(2,1)} %param.12), channel_id=1, replica_groups=mesh['groups'=2,'row'=16] {'row'}, dimensions={1}, use_global_device_ids=true | all-gather | bytes 53312 | tf_op jit(solution)/shard_map/all_gather | solution.py:108
  41.0 2.6 slice_reduce_fusion.48
  43.6 1.6 slice_reduce_fusion.46
  47.8 30.5 %all-reduce.12 = (bf16[512]{0:T(512)(128)(2,1)S(1)}, bf16[512]{0:T(512)(128)(2,1)S(1)}, bf16[512]{0:T(512)(128)(2,1)S(1)}, bf16[512]{0:T(512)(128)(2,1)}) all-reduce(bf16[512]{0:T(512)(128)(2,1)S(1)} %dynamic-update-slice, bf16[512]{0:T(512)(128)(2,1)S(1)} %dynamic-update-slice.2, ...), channel_id=1, replica_groups=mesh['groups'=2,'row'=16] {'row'}, use_global_device_ids=true, to_apply=%add.2 | all-reduce | flops 2048 | bytes 8192
  78.3 2.7 slice_reduce_fusion.47
  81.3 4.4 %collective-permute-start.5 = (bf16[128]{0:T(256)(128)(2,1)S(1)}, bf16[128]{0:T(256)(128)(2,1)S(1)}, u32[]{:S(2)}, u32[]{:S(2)}) collective-permute-start(bf16[128]{0:T(256)(128)(2,1)S(1)} %collective-permute-done.3), channel_id=1, source_target_pairs={{0,15},{1,0},{2,1},{3,2},{4,3},{5,4},{6,5},{7,6},{8,7},{9,8},{10,9... | collective-permute-start | bytes 776 | tf_op jit(solution)/shard_map/ppermute | solution.py:33
  85.7 1.3 collective-permute-done.4
  87.3 4.4 %collective-permute-start.7 = (bf16[128]{0:T(256)(128)(2,1)S(1)}, bf16[128]{0:T(256)(128)(2,1)S(1)}, u32[]{:S(2)}, u32[]{:S(2)}) collective-permute-start(bf16[128]{0:T(256)(128)(2,1)S(1)} %collective-permute-done.5), channel_id=1, source_target_pairs={{0,15},{1,0},{2,1},{3,2},{4,3},{5,4},{6,5},{7,6},{8,7},{9,8},{10,9... | collective-permute-start | bytes 776 | tf_op jit(solution)/shard_map/ppermute | solution.py:33
  93.0 4.4 %collective-permute-start.9 = (bf16[128]{0:T(256)(128)(2,1)S(1)}, bf16[128]{0:T(256)(128)(2,1)S(1)}, u32[]{:S(2)}, u32[]{:S(2)}) collective-permute-start(bf16[128]{0:T(256)(128)(2,1)S(1)} %collective-permute-done.7), channel_id=1, source_target_pairs={{0,15},{1,0},{2,1},{3,2},{4,3},{5,4},{6,5},{7,6},{8,7},{9,8},{10,9... | collective-permute-start | bytes 776 | tf_op jit(solution)/shard_map/ppermute | solution.py:33
  99.0 4.5 %collective-permute-start.11 = (bf16[128]{0:T(256)(128)(2,1)S(1)}, bf16[128]{0:T(256)(128)(2,1)S(1)}, u32[]{:S(2)}, u32[]{:S(2)}) collective-permute-start(bf16[128]{0:T(256)(128)(2,1)S(1)} %collective-permute-done.9), channel_id=1, source_target_pairs={{0,15},{1,0},{2,1},{3,2},{4,3},{5,4},{6,5},{7,6},{8,7},{9,8},{10,9... | collective-permute-start | bytes 776 | tf_op jit(solution)/shard_map/ppermute | solution.py:33
  104.7 4.4 %collective-permute-start.13 = (bf16[128]{0:T(256)(128)(2,1)S(1)}, bf16[128]{0:T(256)(128)(2,1)S(1)}, u32[]{:S(2)}, u32[]{:S(2)}) collective-permute-start(bf16[128]{0:T(256)(128)(2,1)S(1)} %collective-permute-done.11), channel_id=1, source_target_pairs={{0,15},{1,0},{2,1},{3,2},{4,3},{5,4},{6,5},{7,6},{8,7},{9,8},{10,9... | collective-permute-start | bytes 776 | tf_op jit(solution)/shard_map/ppermute | solution.py:33
  110.4 4.4 %collective-permute-start.15 = (bf16[128]{0:T(256)(128)(2,1)S(1)}, bf16[128]{0:T(256)(128)(2,1)S(1)}, u32[]{:S(2)}, u32[]{:S(2)}) collective-permute-start(bf16[128]{0:T(256)(128)(2,1)S(1)} %collective-permute-done.13), channel_id=1, source_target_pairs={{0,15},{1,0},{2,1},{3,2},{4,3},{5,4},{6,5},{7,6},{8,7},{9,8},{10,9... | collective-permute-start | bytes 776 | tf_op jit(solution)/shard_map/ppermute | solution.py:33
  116.3 4.9 %collective-permute-done.16 = bf16[128]{0:T(256)(128)(2,1)S(1)} collective-permute-done((bf16[128]{0:T(256)(128)(2,1)S(1)}, bf16[128]{0:T(256)(128)(2,1)S(1)}, u32[]{:S(2)}, u32[]{:S(2)}) %collective-permute-start.16) | collective-permute-done | bytes 288 | tf_op jit(solution)/shard_map/ppermute | solution.py:26
  121.4 4.7 %fusion.146 = (f32[4,64]{1,0:T(4,128)S(1)}, f32[4,64,512]{2,1,0:T(8,128)S(1)}) fusion(f32[512]{0:T(512)S(1)} %convert_element_type.62, f32[512]{0:T(512)S(1)} %get-tuple-element.85, f32[512]{0:T(512)S(1)} %get-tuple-element.86, f32[512]{0:T(512)S(1)} %get-tuple-element.87, f32[512]{0:T(512)S(1)} %get-tuple-element.88, ...), kind=kLoop, calls=%fused_computation.367 | loop fusion | flops 12975872 | bytes 5608448 | tf_op jit(solution)/shard_map/reduce_sum | solution.py:120
  126.8 3.8 %multiply_convert_fusion = (bf16[256,2048]{1,0:T(8,128)(2,1)S(1)}, f32[256,2048]{1,0:T(8,128)}) fusion(f32[2048]{0:T(1024)S(1)} %convert_element_type.66, bf16[256,512]{1,0:T(8,128)(2,1)S(1)} %bitcast.73, bf16[512,2048]{1,0:T(8,128)(2,1)} %all-gather.3.cloned.1.call-done), kind=kOutput, calls=%fused_computation.60 | convolution fusion | flops 540016640 | bytes 5513216 | tf_op jit(solution)/shard_map/dot_general | solution.py:129
  130.5 4.3 %convert_reduce_fusion.1 = (f32[2048]{0:T(1024)}, bf16[256,2048]{1,0:T(8,128)(2,1)S(1)}) fusion(f32[256,2048]{1,0:T(8,128)} %get-tuple-element.152, f32[2048]{0:T(1024)S(1)} %convert_element_type.66, bf16[256,512]{1,0:T(8,128)(2,1)} %bitcast.75, bf16[2048,512]{1,0:T(8,128)(2,1)} %all-gather.5.cloned.1.call-done), kind=kOutput, calls=%fused_computation.59 | convolution fusion | flops 543684608 | bytes 5521408 | tf_op jit(solution)/shard_map/dot_general | solution.py:150
  134.9 1.3 fusion.145
  139.1 3.2 fusion.143
  142.2 1.4 fusion.142
  145.0 2.3 stack.199
  148.4 3.9 %convolution_multiply_fusion.1 = f32[512,2048]{1,0:T(8,128)} fusion(bf16[256,512]{1,0:T(8,128)(2,1)S(1)} %bitcast.74, bf16[256,2048]{1,0:T(8,128)(2,1)} %copy-done.6), kind=kOutput, calls=%fused_computation.51 | convolution fusion | flops 537919488 | bytes 5505024 | tf_op jit(solution)/shard_map/dot_general | solution.py:159
  153.3 2.7 convolution_multiply_fusion
  157.5 57.6 %all-reduce.11 = (f32[512]{0:T(512)S(1)}, f32[512]{0:T(512)S(1)}, f32[512]{0:T(512)S(1)}, f32[2048]{0:T(1024)S(1)}, f32[512]{0:T(512)S(1)}) all-reduce(f32[512]{0:T(512)S(1)} %broadcast_multiply_fusion.5, f32[512]{0:T(512)S(1)} %get-tuple-element.157, ...), channel_id=5, replica_groups=mesh['groups'=2,'row'=16] {'row'}, use_global_device_ids=true, to_apply=%region_57.58.clone | all-reduce | flops 4096 | bytes 32768
  217.5 1.3 collective-permute-start.17
  218.8 1.3 collective-permute-start.18
  220.7 2.4 convolution_add_fusion
  224.3 4.7 %fusion.5 = bf16[4,64,512]{2,1,0:T(8,128)(2,1)} fusion(bf16[4,64,512]{2,1,0:T(8,128)(2,1)S(1)} %copy-done.4, f32[10,64,512]{2,1,0:T(8,128)S(1)} %maximum_convert_fusion.1, f32[512]{0:T(512)S(1)} %get-tuple-element.85, f32[512]{0:T(512)S(1)} %get-tuple-element.86, f32[512]{0:T(512)S(1)} %get-tuple-element.87, f32[512]{0:T(512)S(1)} %get-tuple-element.88, ...), kind=kLoop, calls=%fused_computation.151 | loop fusion | flops 13107200 | bytes 5605376 | tf_op jit(solution)/shard_map/convert_element_type | solution.py:196
  229.0 48.3 %reduce-scatter.6.cloned.1.call-done = f32[32,2048]{1,0:T(8,128)} async-done(((f32[512,2048]{1,0:T(8,128)}), f32[32,2048]{1,0:T(8,128)}) %reduce-scatter.6.cloned.1.call-update) | async-done | bytes 262160 | tf_op jit(solution)/shard_map/reduce_scatter | solution.py:158
  277.3 76.0 %reduce-scatter.8.cloned.1.call-done = f32[128,512]{1,0:T(8,128)} async-done(((f32[2048,512]{1,0:T(8,128)}), f32[128,512]{1,0:T(8,128)}) %reduce-scatter.8.cloned.1.call-update) | async-done | bytes 262160 | tf_op jit(solution)/shard_map/reduce_scatter | solution.py:149
  (236 shorter events, 22.9 us)
Async XLA Ops:
  7.2 119.6 %all-gather.3.cloned.1.call-start = ((), (), s32[]{:S(2)}) async-start(), calls=%async_computation.3 | async-start | bytes 2228224 | tf_op jit(solution)/shard_map/all_gather | solution.py:131
  7.9 122.6 %all-gather.5.cloned.1.call-start = ((), (), s32[]{:S(2)}) async-start(), calls=%async_computation.4 | async-start | bytes 2228224 | tf_op jit(solution)/shard_map/all_gather | solution.py:138
  8.7 220.3 %reduce-scatter.10.cloned.1.call-start = ((), (), s32[]{:S(2)}) async-start(), calls=%async_computation.7 | async-start | bytes 278528
  8.7 72.5 %collective-permute-start.2 = (bf16[128]{0:T(256)(128)(2,1)}, bf16[128]{0:T(256)(128)(2,1)S(1)}, u32[]{:S(2)}, u32[]{:S(2)}) collective-permute-start(bf16[128]{0:T(256)(128)(2,1)} %param.17), channel_id=1, source_target_pairs={{0,1},{1,2},{2,3},{3,4},{4,5},{5,6},{6,7},{7,8},{8,9},{9,10},{10,1... | collective-permute-start | bytes 776 | tf_op jit(solution)/shard_map/ppermute | solution.py:26
  9.2 72.0 %collective-permute-start.3 = (bf16[128]{0:T(256)(128)(2,1)}, bf16[128]{0:T(256)(128)(2,1)S(1)}, u32[]{:S(2)}, u32[]{:S(2)}) collective-permute-start(bf16[128]{0:T(256)(128)(2,1)} %param.17), channel_id=1, source_target_pairs={{0,15},{1,0},{2,1},{3,2},{4,3},{5,4},{6,5},{7,6},{8,7},{9,8},{10,9... | collective-permute-start | bytes 776 | tf_op jit(solution)/shard_map/ppermute | solution.py:33
  15.3 106.0 %collective-permute-start = (bf16[3,64,512]{2,1,0:T(8,128)(2,1)S(1)}, bf16[3,64,512]{2,1,0:T(8,128)(2,1)S(1)}, u32[]{:S(2)}, u32[]{:S(2)}) collective-permute-start(bf16[3,64,512]{2,1,0:T(8,128)(2,1)S(1)} %get-tuple-element.147), channel_id=1, source_target_pairs={{0,1},{1,2},{2,3},{3,4},{4,5},{5,6},{6,7},{7,8},{8,9},{9,10},{10,1... | collective-permute-start | bytes 589832 | tf_op jit(solution)/shard_map/ppermute | solution.py:49
  16.7 104.7 %collective-permute-start.1 = (bf16[3,64,512]{2,1,0:T(8,128)(2,1)S(1)}, bf16[3,64,512]{2,1,0:T(8,128)(2,1)S(1)}, u32[]{:S(2)}, u32[]{:S(2)}) collective-permute-start(bf16[3,64,512]{2,1,0:T(8,128)(2,1)S(1)} %get-tuple-element.148), channel_id=1, source_target_pairs={{1,0},{2,1},{3,2},{4,3},{5,4},{6,5},{7,6},{8,7},{9,8},{10,9},{11,1... | collective-permute-start | bytes 589832 | tf_op jit(solution)/shard_map/ppermute | solution.py:52
  81.0 45.2 %copy-start.7 = (f32[512]{0:T(512)}, f32[512]{0:T(512)S(1)}, u32[]{:S(2)}) copy-start(f32[512]{0:T(512)S(1)} %get-tuple-element.104) | copy-start | bytes 6148
  81.0 45.2 %copy-start.9 = (f32[512]{0:T(512)}, f32[512]{0:T(512)S(1)}, u32[]{:S(2)}) copy-start(f32[512]{0:T(512)S(1)} %get-tuple-element.105) | copy-start | bytes 6148
  81.0 45.2 %copy-start.11 = (f32[512]{0:T(512)}, f32[512]{0:T(512)S(1)}, u32[]{:S(2)}) copy-start(f32[512]{0:T(512)S(1)} %get-tuple-element.106) | copy-start | bytes 6148
  81.0 45.2 %copy-start.13 = (f32[512]{0:T(512)}, f32[512]{0:T(512)S(1)}, u32[]{:S(2)}) copy-start(f32[512]{0:T(512)S(1)} %get-tuple-element.107) | copy-start | bytes 6148
  81.0 45.2 %copy-start.15 = (f32[512]{0:T(512)}, f32[512]{0:T(512)S(1)}, u32[]{:S(2)}) copy-start(f32[512]{0:T(512)S(1)} %get-tuple-element.108) | copy-start | bytes 6148
  81.0 45.2 %copy-start.17 = (f32[512]{0:T(512)}, f32[512]{0:T(512)S(1)}, u32[]{:S(2)}) copy-start(f32[512]{0:T(512)S(1)} %get-tuple-element.109) | copy-start | bytes 6148
  81.1 45.2 %copy-start.19 = (f32[512]{0:T(512)}, f32[512]{0:T(512)S(1)}, u32[]{:S(2)}) copy-start(f32[512]{0:T(512)S(1)} %get-tuple-element.110) | copy-start | bytes 6148
  81.1 45.2 %copy-start.21 = (f32[512]{0:T(512)}, f32[512]{0:T(512)S(1)}, u32[]{:S(2)}) copy-start(f32[512]{0:T(512)S(1)} %get-tuple-element.111) | copy-start | bytes 6148
  81.2 5.8 %collective-permute-start.4 = (bf16[128]{0:T(256)(128)(2,1)S(1)}, bf16[128]{0:T(256)(128)(2,1)S(1)}, u32[]{:S(2)}, u32[]{:S(2)}) collective-permute-start(bf16[128]{0:T(256)(128)(2,1)S(1)} %collective-permute-done.2), channel_id=1, source_target_pairs={{0,1},{1,2},{2,3},{3,4},{4,5},{5,6},{6,7},{7,8},{8,9},{9,10},{10,1... | collective-permute-start | bytes 776 | tf_op jit(solution)/shard_map/ppermute | solution.py:26
  81.3 5.9 %collective-permute-start.5 = (bf16[128]{0:T(256)(128)(2,1)S(1)}, bf16[128]{0:T(256)(128)(2,1)S(1)}, u32[]{:S(2)}, u32[]{:S(2)}) collective-permute-start(bf16[128]{0:T(256)(128)(2,1)S(1)} %collective-permute-done.3), channel_id=1, source_target_pairs={{0,15},{1,0},{2,1},{3,2},{4,3},{5,4},{6,5},{7,6},{8,7},{9,8},{10,9... | collective-permute-start | bytes 776 | tf_op jit(solution)/shard_map/ppermute | solution.py:33
  87.0 5.7 %collective-permute-start.6 = (bf16[128]{0:T(256)(128)(2,1)S(1)}, bf16[128]{0:T(256)(128)(2,1)S(1)}, u32[]{:S(2)}, u32[]{:S(2)}) collective-permute-start(bf16[128]{0:T(256)(128)(2,1)S(1)} %collective-permute-done.4), channel_id=1, source_target_pairs={{0,1},{1,2},{2,3},{3,4},{4,5},{5,6},{6,7},{7,8},{8,9},{9,10},{10,1... | collective-permute-start | bytes 776 | tf_op jit(solution)/shard_map/ppermute | solution.py:26
  87.3 5.7 %collective-permute-start.7 = (bf16[128]{0:T(256)(128)(2,1)S(1)}, bf16[128]{0:T(256)(128)(2,1)S(1)}, u32[]{:S(2)}, u32[]{:S(2)}) collective-permute-start(bf16[128]{0:T(256)(128)(2,1)S(1)} %collective-permute-done.5), channel_id=1, source_target_pairs={{0,15},{1,0},{2,1},{3,2},{4,3},{5,4},{6,5},{7,6},{8,7},{9,8},{10,9... | collective-permute-start | bytes 776 | tf_op jit(solution)/shard_map/ppermute | solution.py:33
  92.7 5.7 %collective-permute-start.8 = (bf16[128]{0:T(256)(128)(2,1)S(1)}, bf16[128]{0:T(256)(128)(2,1)S(1)}, u32[]{:S(2)}, u32[]{:S(2)}) collective-permute-start(bf16[128]{0:T(256)(128)(2,1)S(1)} %collective-permute-done.6), channel_id=1, source_target_pairs={{0,1},{1,2},{2,3},{3,4},{4,5},{5,6},{6,7},{7,8},{8,9},{9,10},{10,1... | collective-permute-start | bytes 776 | tf_op jit(solution)/shard_map/ppermute | solution.py:26
  93.0 6.0 %collective-permute-start.9 = (bf16[128]{0:T(256)(128)(2,1)S(1)}, bf16[128]{0:T(256)(128)(2,1)S(1)}, u32[]{:S(2)}, u32[]{:S(2)}) collective-permute-start(bf16[128]{0:T(256)(128)(2,1)S(1)} %collective-permute-done.7), channel_id=1, source_target_pairs={{0,15},{1,0},{2,1},{3,2},{4,3},{5,4},{6,5},{7,6},{8,7},{9,8},{10,9... | collective-permute-start | bytes 776 | tf_op jit(solution)/shard_map/ppermute | solution.py:33
  98.4 5.7 %collective-permute-start.10 = (bf16[128]{0:T(256)(128)(2,1)S(1)}, bf16[128]{0:T(256)(128)(2,1)S(1)}, u32[]{:S(2)}, u32[]{:S(2)}) collective-permute-start(bf16[128]{0:T(256)(128)(2,1)S(1)} %collective-permute-done.8), channel_id=1, source_target_pairs={{0,1},{1,2},{2,3},{3,4},{4,5},{5,6},{6,7},{7,8},{8,9},{9,10},{10,1... | collective-permute-start | bytes 776 | tf_op jit(solution)/shard_map/ppermute | solution.py:26
  99.0 5.8 %collective-permute-start.11 = (bf16[128]{0:T(256)(128)(2,1)S(1)}, bf16[128]{0:T(256)(128)(2,1)S(1)}, u32[]{:S(2)}, u32[]{:S(2)}) collective-permute-start(bf16[128]{0:T(256)(128)(2,1)S(1)} %collective-permute-done.9), channel_id=1, source_target_pairs={{0,15},{1,0},{2,1},{3,2},{4,3},{5,4},{6,5},{7,6},{8,7},{9,8},{10,9... | collective-permute-start | bytes 776 | tf_op jit(solution)/shard_map/ppermute | solution.py:33
  104.1 5.7 %collective-permute-start.12 = (bf16[128]{0:T(256)(128)(2,1)S(1)}, bf16[128]{0:T(256)(128)(2,1)S(1)}, u32[]{:S(2)}, u32[]{:S(2)}) collective-permute-start(bf16[128]{0:T(256)(128)(2,1)S(1)} %collective-permute-done.10), channel_id=1, source_target_pairs={{0,1},{1,2},{2,3},{3,4},{4,5},{5,6},{6,7},{7,8},{8,9},{9,10},{10,1... | collective-permute-start | bytes 776 | tf_op jit(solution)/shard_map/ppermute | solution.py:26
  104.7 5.7 %collective-permute-start.13 = (bf16[128]{0:T(256)(128)(2,1)S(1)}, bf16[128]{0:T(256)(128)(2,1)S(1)}, u32[]{:S(2)}, u32[]{:S(2)}) collective-permute-start(bf16[128]{0:T(256)(128)(2,1)S(1)} %collective-permute-done.11), channel_id=1, source_target_pairs={{0,15},{1,0},{2,1},{3,2},{4,3},{5,4},{6,5},{7,6},{8,7},{9,8},{10,9... | collective-permute-start | bytes 776 | tf_op jit(solution)/shard_map/ppermute | solution.py:33
  109.8 5.7 %collective-permute-start.14 = (bf16[128]{0:T(256)(128)(2,1)S(1)}, bf16[128]{0:T(256)(128)(2,1)S(1)}, u32[]{:S(2)}, u32[]{:S(2)}) collective-permute-start(bf16[128]{0:T(256)(128)(2,1)S(1)} %collective-permute-done.12), channel_id=1, source_target_pairs={{0,1},{1,2},{2,3},{3,4},{4,5},{5,6},{6,7},{7,8},{8,9},{9,10},{10,1... | collective-permute-start | bytes 776 | tf_op jit(solution)/shard_map/ppermute | solution.py:26
  110.4 5.7 %collective-permute-start.15 = (bf16[128]{0:T(256)(128)(2,1)S(1)}, bf16[128]{0:T(256)(128)(2,1)S(1)}, u32[]{:S(2)}, u32[]{:S(2)}) collective-permute-start(bf16[128]{0:T(256)(128)(2,1)S(1)} %collective-permute-done.13), channel_id=1, source_target_pairs={{0,15},{1,0},{2,1},{3,2},{4,3},{5,4},{6,5},{7,6},{8,7},{9,8},{10,9... | collective-permute-start | bytes 776 | tf_op jit(solution)/shard_map/ppermute | solution.py:33
  115.4 5.7 %collective-permute-start.16 = (bf16[128]{0:T(256)(128)(2,1)S(1)}, bf16[128]{0:T(256)(128)(2,1)S(1)}, u32[]{:S(2)}, u32[]{:S(2)}) collective-permute-start(bf16[128]{0:T(256)(128)(2,1)S(1)} %collective-permute-done.14), channel_id=1, source_target_pairs={{0,1},{1,2},{2,3},{3,4},{4,5},{5,6},{6,7},{7,8},{8,9},{9,10},{10,1... | collective-permute-start | bytes 776 | tf_op jit(solution)/shard_map/ppermute | solution.py:26
  148.2 129.1 %reduce-scatter.6.cloned.1.call-start = ((), (), s32[]{:S(2)}) async-start(), calls=%async_computation.5 | async-start | bytes 4456448 | tf_op jit(solution)/shard_map/reduce_scatter | solution.py:158
  152.3 200.9 %reduce-scatter.8.cloned.1.call-start = ((), (), s32[]{:S(2)}) async-start(), calls=%async_computation.6 | async-start | bytes 4456448 | tf_op jit(solution)/shard_map/reduce_scatter | solution.py:149
  217.5 6.6 %collective-permute-start.17 = (bf16[3,64,512]{2,1,0:T(8,128)(2,1)S(1)}, bf16[3,64,512]{2,1,0:T(8,128)(2,1)S(1)}, u32[]{:S(2)}, u32[]{:S(2)}) collective-permute-start(bf16[3,64,512]{2,1,0:T(8,128)(2,1)S(1)} %get-tuple-element.145), channel_id=1, source_target_pairs={{0,1},{1,2},{2,3},{3,4},{4,5},{5,6},{6,7},{7,8},{8,9},{9,10},{10,1... | collective-permute-start | bytes 589832 | tf_op jit(solution)/shard_map/ppermute | solution.py:49
  218.8 5.2 %collective-permute-start.18 = (bf16[3,64,512]{2,1,0:T(8,128)(2,1)S(1)}, bf16[3,64,512]{2,1,0:T(8,128)(2,1)S(1)}, u32[]{:S(2)}, u32[]{:S(2)}) collective-permute-start(bf16[3,64,512]{2,1,0:T(8,128)(2,1)S(1)} %get-tuple-element.146), channel_id=1, source_target_pairs={{1,0},{2,1},{3,2},{4,3},{5,4},{6,5},{7,6},{8,7},{9,8},{10,9},{11,1... | collective-permute-start | bytes 589832 | tf_op jit(solution)/shard_map/ppermute | solution.py:52
  (62 other events, 582.8 us)
Sparse Core Ops, SparseCore 0:
  10.1 44.7 all-gather.2
  57.1 40.2 all-gather.4
  148.3 52.8 reduce-scatter.9
  205.4 71.7 reduce-scatter.5
  281.6 71.6 reduce-scatter.7
